TPU v7x, 32 devices: a whole 2x2x4 slice. The times are simulated.
32 devices in a mesh: groups: 2 (over x), frame: 16 (over z, y, core).
Axes of the slice: x: 2, y: 2, z: 4, core: 2. Of those that a mesh axis runs over, the one named last changes fastest.
Arguments:
- lowres: bfloat16 [32, 64, 128], P(('groups', 'frame')), parts along dimension 0, may hold values from -6 to 6
- noisy: bfloat16 [32, 8, 64, 128], P(('groups', 'frame')), parts along dimension 0, may hold values from -6 to 6
- starts: int32 [8], P('groups'), parts along dimension 0, may hold values from 0 to 8, as said below
- blend: int32 [8, 8], P('groups'), parts along dimension 0, may hold values from 1 to 4
- assign: int32 [32], P('groups'), parts along dimension 0, may hold values from 0 to 15, each once
- base_w: bfloat16 [3, 128, 128], replicated, may hold values from -0.3125 to 0.3125
- cond_w: bfloat16 [128, 128], replicated, may hold values from -0.5 to 0.5
- noise_w: bfloat16 [128, 128], replicated, may hold values from -0.5 to 0.5
- gains: float32 [3, 128], replicated, may hold values from 0.25 to 1.75
- tconv: float32 [3, 3, 128], replicated, may hold values from -3 to 3
- mlp_in: bfloat16 [3, 128, 512], replicated, may hold values from -0.5 to 0.5
- mlp_out: bfloat16 [3, 512, 128], replicated, may hold values from -0.25 to 0.25
Outputs:
- video: bfloat16 [32, 256, 128], P(('groups', 'frame')), parts along dimension 0
There are 2 independent parts, one for each index of `groups`. A program takes and returns all parts, laid end to end along the dimension named above; an argument that names none is the same for every part. Nothing has to cross between parts.
Inputs may be any that keep to these rules, and one draw needn't show every extreme that they name: Window k covers frames starts[k] to starts[k] + 7; every frame lies in some window; the first window starts at 0 and the last at 8.
All inputs are finite; a program needn't handle non-finite values.
Results may differ from a plain program's by a relative error of at most 0.0059.
Values may be sent and summed in bfloat16 or wider, within the bound.
No kernel may reach another device: no remote copies, remote signals or barrier semaphores. Data moves between devices by JAX's collectives and lax.ppermute only.
A program may use at most 64 MiB of HBM per device.

v0:
```python
import jax
import jax.numpy as jnp
from jax import lax
from jax.sharding import PartitionSpec as P

TILES = 4


def padded_2(cells, sides, width):
    for axis, dim in sides:
        count = lax.axis_size(axis)
        ends = count - 1
        head = lax.slice_in_dim(cells, 0, width, axis=dim)
        tail = lax.slice_in_dim(cells, cells.shape[dim] - width, cells.shape[dim], axis=dim)
        cells = jnp.concatenate(
            [
                lax.ppermute(tail, axis, [(i, (i + 1) % count) for i in range(ends)]),
                cells,
                lax.ppermute(head, axis, [((i + 1) % count, i) for i in range(ends)]),
            ],
            axis=dim,
        )
    return cells


def refine_block(cond, noisy_item, cond_w, noise_w, gains, tconv, mlp_in, mlp_out):
    frame_count, positions, channels = cond.shape
    row_count = frame_count * positions
    state = jnp.dot(cond.reshape(row_count, channels), cond_w, preferred_element_type=jnp.float32)
    state = state + jnp.dot(
        noisy_item.reshape(row_count, channels), noise_w, preferred_element_type=jnp.float32
    )
    for layer_id in range(gains.shape[0]):
        inverse = lax.rsqrt(jnp.mean(state * state, axis=-1, keepdims=True) + 1e-06)
        normed = (state * inverse * gains[layer_id]).reshape(frame_count, positions, channels)
        zeros_frame = jnp.zeros_like(normed[:1])
        before = jnp.concatenate([zeros_frame, normed[:-1]], 0)
        behind = jnp.concatenate([normed[1:], zeros_frame], 0)
        mixed_rows = (
            normed
            + tconv[layer_id, 0] * before
            + tconv[layer_id, 1] * normed
            + tconv[layer_id, 2] * behind
        )
        mixed_rows = mixed_rows.reshape(row_count, channels).astype(jnp.bfloat16)
        hidden = jax.nn.silu(
            jnp.dot(mixed_rows, mlp_in[layer_id], preferred_element_type=jnp.float32)
        ).astype(jnp.bfloat16)
        state = state + jnp.dot(hidden, mlp_out[layer_id], preferred_element_type=jnp.float32)
    return state.astype(jnp.bfloat16).reshape(frame_count, positions, channels)


def refine(cond, noisy_item, cond_w, noise_w, gains, tconv, mlp_in, mlp_out):
    frame_count, positions, channels = cond.shape
    block_count = positions // positions
    cond_blocks = jnp.transpose(
        cond.reshape(frame_count, block_count, positions, channels), (1, 0, 2, 3)
    )
    noisy_blocks = jnp.transpose(
        noisy_item.reshape(frame_count, block_count, positions, channels), (1, 0, 2, 3)
    )

    def one_block(pair):
        return refine_block(pair[0], pair[1], cond_w, noise_w, gains, tconv, mlp_in, mlp_out)

    outputs = lax.map(one_block, (cond_blocks, noisy_blocks))
    return jnp.transpose(outputs, (1, 0, 2, 3)).reshape(frame_count, positions, channels)


def on_device(
    lowres, noisy, starts, blend, assign, base_w, cond_w, noise_w, gains, tconv, mlp_in, mlp_out
):
    frame_total = assign.shape[0]
    window_len = noisy.shape[1]
    tile_pos = noisy.shape[2]
    channels = noisy.shape[3]
    low_pos = lowres.shape[1] // TILES
    padded = padded_2(lowres, (("frame", 0),), 1)
    total = jnp.dot(padded[0], base_w[0], preferred_element_type=jnp.float32)
    total = total + jnp.dot(padded[1], base_w[1], preferred_element_type=jnp.float32)
    total = total + jnp.dot(padded[2], base_w[2], preferred_element_type=jnp.float32)
    base_frame = (lowres[0].astype(jnp.float32) + jax.nn.silu(total)).astype(jnp.bfloat16)
    own_index = lax.axis_index("frame")
    item_id = assign[own_index]
    own_start = starts[item_id // TILES]
    tile_rows = base_frame.reshape(TILES, low_pos * channels)
    picker = (assign[:, None] % TILES == jnp.arange(TILES, dtype=jnp.int32)[None, :]).astype(
        jnp.bfloat16
    )
    outgoing = jnp.dot(picker, tile_rows, preferred_element_type=jnp.float32).astype(jnp.bfloat16)
    outgoing = outgoing.reshape(frame_total, low_pos, channels)
    gathered = lax.all_to_all(outgoing, "frame", split_axis=0, concat_axis=0, tiled=True)
    window_tiles = lax.dynamic_slice_in_dim(gathered, own_start, window_len, 0)
    cond = jnp.repeat(window_tiles, 4, axis=1)
    refined = refine(cond, noisy[0], cond_w, noise_w, gains, tconv, mlp_in, mlp_out)
    source_window = assign // TILES
    source_tile = assign % TILES
    placed = jnp.zeros((frame_total, tile_pos, channels), jnp.bfloat16)
    placed = lax.dynamic_update_slice_in_dim(placed, refined, own_start, 0)
    received = lax.all_to_all(placed, "frame", split_axis=0, concat_axis=0, tiled=True)
    offset = own_index - starts[source_window]
    inside = (offset >= 0) & (offset < window_len)
    clipped = jnp.clip(offset, 0, window_len - 1)
    factor = jnp.where(inside, blend[source_window, clipped], 0).astype(jnp.float32)
    tile_match = (source_tile[None, :] == jnp.arange(TILES, dtype=jnp.int32)[:, None]).astype(
        jnp.float32
    )
    blend_matrix = tile_match * factor[None, :]
    weighted = jnp.dot(
        blend_matrix.astype(jnp.bfloat16),
        received.reshape(frame_total, tile_pos * channels),
        preferred_element_type=jnp.float32,
    )
    denom = jnp.sum(blend_matrix, axis=1)
    video = weighted / denom[:, None]
    return video.reshape(1, TILES * tile_pos, channels).astype(jnp.bfloat16)


def solution(mesh):
    in_specs = (
        P(("groups", "frame"), None, None),
        P(("groups", "frame"), None, None, None),
        P("groups"),
        P("groups", None),
        P("groups"),
        P(),
        P(),
        P(),
        P(),
        P(),
        P(),
        P(),
    )
    out_specs = P(("groups", "frame"), None, None)
    return jax.shard_map(
        on_device, mesh=mesh, in_specs=in_specs, out_specs=out_specs, check_vma=False
    )
```

profile of v0, /device:TPU:0, one launch (start us, length us, event | category | flops | bytes accessed | tf_op | source)
XLA Modules:
  0.0 52.0 jit_solution(3728004417824354756)
XLA Ops:
  0.0 1.4 %collective-permute-start.1 = (bf16[1,64,128]{2,1,0:T(8,128)(2,1)}, bf16[1,64,128]{2,1,0:T(8,128)(2,1)S(1)}, u32[]{:S(2)}, u32[]{:S(2)}) collective-permute-start(bf16[1,64,128]{2,1,0:T(8,128)(2,1)} %param.12), channel_id=1, source_target_pairs={{1,0},{2,1},{3,2},{4,3},{5,4},{6,5},{7,6},{8,7},{9,8},{10,9},{11,1... | collective-permute-start | bytes 49160 | tf_op jit(solution)/shard_map/ppermute | solution.py:19
  1.4 3.0 %collective-permute-start = (bf16[1,64,128]{2,1,0:T(8,128)(2,1)}, bf16[1,64,128]{2,1,0:T(8,128)(2,1)S(1)}, u32[]{:S(2)}, u32[]{:S(2)}) collective-permute-start(bf16[1,64,128]{2,1,0:T(8,128)(2,1)} %param.12), channel_id=1, source_target_pairs={{0,1},{1,2},{2,3},{3,4},{4,5},{5,6},{6,7},{7,8},{8,9},{9,10},{10,1... | collective-permute-start | bytes 49160 | tf_op jit(solution)/shard_map/ppermute | solution.py:17
  4.5 0.7 %compare_select_fusion.1 = (s32[16]{0:T(128)S(1)}, s32[16]{0:T(128)S(1)}) fusion(s32[16]{0:T(128)} %param.16), kind=kLoop, calls=%fused_computation.58 | loop fusion | flops 352 | bytes 192 | tf_op jit(solution)/shard_map/select_n | solution.py:101
  5.1 0.9 %fusion.29 = f32[64,128]{1,0:T(8,128)S(1)} fusion(bf16[3,128,128]{2,1,0:T(8,128)(2,1)} %param.17, bf16[1,64,128]{2,1,0:T(8,128)(2,1)} %param.12), kind=kOutput, calls=%fused_computation.44 | convolution fusion | flops 2097152 | bytes 81920 | tf_op jit(solution)/shard_map/dot_general | solution.py:80
  6.1 0.6 %copy-done.11 = s32[16]{0:T(128)S(1)} copy-done((s32[16]{0:T(128)S(1)}, s32[16]{0:T(128)}, u32[]{:S(2)}) %copy-start.11) | copy-done | bytes 88
  6.7 0.6 %dynamic_slice.14 = s32[1]{0:T(128)} dynamic-slice(s32[16]{0:T(128)S(1)} %copy-done.11, s32[]{:T(128)S(6)} %select_n.58), dynamic_slice_sizes={1} | dynamic-slice | bytes 12 | tf_op jit(solution)/shard_map/dynamic_slice | solution.py:84
  9.9 0.6 %copy-done.1 = s32[4]{0:T(128)S(1)} copy-done((s32[4]{0:T(128)S(1)}, s32[4]{0:T(128)}, u32[]{:S(2)}) %copy-start.1) | copy-done | bytes 40
  10.6 0.6 %dynamic_slice.15 = s32[1]{0:T(128)} dynamic-slice(s32[4]{0:T(128)S(1)} %copy-done.1, s32[]{:T(128)S(6)} %select_n.60), dynamic_slice_sizes={1} | dynamic-slice | bytes 12 | tf_op jit(solution)/shard_map/dynamic_slice | solution.py:85
  12.5 0.7 %gather_fusion = s32[16]{0:T(128)S(1)} fusion(s32[4]{0:T(128)S(1)} %copy-done.1, s32[1024]{0:T(1024)S(1)} %pad_clamp_fusion), kind=kCustom, calls=%fused_computation | custom fusion | bytes 192 | tf_op jit(solution)/shard_map/gather | solution.py:101
  14.0 0.6 %copy-done.6 = bf16[1,64,128]{2,1,0:T(8,128)(2,1)S(1)} copy-done((bf16[1,64,128]{2,1,0:T(8,128)(2,1)S(1)}, bf16[1,64,128]{2,1,0:T(8,128)(2,1)}, u32[]{:S(2)}) %copy-start.6) | copy-done | bytes 16408
  14.5 0.1 add_convert_fusion.3
  14.7 0.2 fusion.2
  14.9 0.6 %copy.13 = bf16[2,8,16,128]{3,2,1,0:T(8,128)(2,1)} copy(bf16[2,8,16,128]{3,1,2,0:T(8,128)(2,1)S(1)} %fusion.2) | data formatting | bytes 131072
  15.6 8.1 %all-to-all-start = ((bf16[16,16,128]{2,1,0:T(8,128)(2,1)}), bf16[16,16,128]{2,1,0:T(8,128)(2,1)S(1)}, u32[]{:S(2)}, u32[]{:S(2)}) async-start(bf16[16,16,128]{2,1,0:T(8,128)(2,1)} %bitcast.45), calls=%async_computation | async-start | bytes 131072 | tf_op jit(solution)/shard_map/all_to_all | solution.py:92
  23.7 6.9 %all-to-all-done = bf16[16,16,128]{2,1,0:T(8,128)(2,1)S(1)} async-done(((bf16[16,16,128]{2,1,0:T(8,128)(2,1)}), bf16[16,16,128]{2,1,0:T(8,128)(2,1)S(1)}, u32[]{:S(2)}, u32[]{:S(2)}) %all-to-all-start) | async-done | bytes 65568 | tf_op jit(solution)/shard_map/all_to_all | solution.py:92
  30.6 0.7 %copy-done.4 = bf16[128,128]{1,0:T(8,128)(2,1)S(1)} copy-done((bf16[128,128]{1,0:T(8,128)(2,1)S(1)}, bf16[128,128]{1,0:T(8,128)(2,1)}, u32[]{:S(2)}) %copy-start.4) | copy-done | bytes 32792
  31.3 0.2 fusion.60
  31.5 0.6 %copy-done.5 = bf16[128,128]{1,0:T(8,128)(2,1)S(1)} copy-done((bf16[128,128]{1,0:T(8,128)(2,1)S(1)}, bf16[128,128]{1,0:T(8,128)(2,1)}, u32[]{:S(2)}) %copy-start.5) | copy-done | bytes 32792
  32.1 0.3 multiply_reduce_fusion.2
  32.4 0.1 multiply_multiply_fusion.2
  32.7 0.9 %copy-done.9 = bf16[3,512,128]{2,1,0:T(8,128)(2,1)S(1)} copy-done((bf16[3,512,128]{2,1,0:T(8,128)(2,1)S(1)}, bf16[3,512,128]{2,1,0:T(8,128)(2,1)}, u32[]{:S(2)}) %copy-start.9) | copy-done | bytes 393240
  33.7 0.6 %multiply_reduce_fusion.1 = (f32[512]{0:T(512)S(1)}, f32[512,128]{1,0:T(8,128)S(1)}) fusion(f32[512,128]{1,0:T(8,128)S(1)} %get-tuple-element.56, bf16[3,512,128]{2,1,0:T(8,128)(2,1)S(1)} %copy-done.9, bf16[512,128]{1,0:T(8,128)(2,1)S(1)} %bitcast.129, bf16[3,128,512]{2,1,0:T(8,128)(2,1)S(1)} %copy-done.10), kind=kOutput, calls=%fused_computation.26 | convolution fusion | flops 135724544 | bytes 919552 | tf_op jit(solution)/shard_map/while/body/eval_jaxpr/dot_general | solution.py:49
  34.6 0.6 %multiply_reduce_fusion = (f32[512]{0:T(512)S(1)}, f32[512,128]{1,0:T(8,128)S(1)}) fusion(f32[512,128]{1,0:T(8,128)S(1)} %get-tuple-element.58, bf16[3,512,128]{2,1,0:T(8,128)(2,1)S(1)} %copy-done.9, bf16[512,128]{1,0:T(8,128)(2,1)S(1)} %bitcast.130, bf16[3,128,512]{2,1,0:T(8,128)(2,1)S(1)} %copy-done.10), kind=kOutput, calls=%fused_computation.23 | convolution fusion | flops 135724544 | bytes 919552 | tf_op jit(solution)/shard_map/while/body/eval_jaxpr/dot_general | solution.py:49
  35.6 0.6 %fusion.1 = bf16[512,128]{1,0:T(8,128)(2,1)S(1)} fusion(f32[512,128]{1,0:T(8,128)S(1)} %get-tuple-element.60, bf16[512,128]{1,0:T(8,128)(2,1)S(1)} %bitcast.131, bf16[3,512,128]{2,1,0:T(8,128)(2,1)S(1)} %copy-done.9, bf16[3,128,512]{2,1,0:T(8,128)(2,1)S(1)} %copy-done.10), kind=kOutput, calls=%fused_computation.9 | convolution fusion | flops 135659520 | bytes 786432 | tf_op jit(solution)/shard_map/while/body/eval_jaxpr/dot_general | solution.py:49
  36.1 0.8 %broadcast_in_dim.18 = bf16[16,64,128]{2,1,0:T(8,128)(2,1)} broadcast(bf16[]{:T(256)} %constant.86.clone.1), dimensions={} | broadcast | bytes 262146 | tf_op jit(solution)/shard_map/broadcast_in_dim | solution.py:98
  36.9 0.7 %constant_dynamic-update-slice_fusion = bf16[16,64,128]{2,1,0:T(8,128)(2,1)} fusion(bf16[16,64,128]{2,1,0:T(8,128)(2,1)} %broadcast_in_dim.18, bf16[8,64,128]{2,1,0:T(8,128)(2,1)S(1)} %bitcast.128, s32[]{:T(128)S(6)} %select_n.61), kind=kLoop, calls=%fused_computation.89 | loop fusion | bytes 262148 | tf_op jit(solution)/shard_map/dynamic_update_slice | solution.py:99
  37.5 3.5 %all-to-all-start.1 = ((bf16[16,64,128]{2,1,0:T(8,128)(2,1)}), bf16[16,64,128]{2,1,0:T(8,128)(2,1)S(1)}, u32[]{:S(2)}, u32[]{:S(2)}) async-start(bf16[16,64,128]{2,1,0:T(8,128)(2,1)} %constant_dynamic-update-slice_fusion), calls=%async_computation.1 | async-start | bytes 524288 | tf_op jit(solution)/shard_map/all_to_all | solution.py:100
  41.1 0.7 %copy-done.2 = s32[4,8]{1,0:T(4,128)S(1)} copy-done((s32[4,8]{1,0:T(4,128)S(1)}, s32[4,8]{1,0:T(4,128)}, u32[]{:S(2)}) %copy-start.2) | copy-done | bytes 152
  41.7 0.7 %gather_fusion.1 = s32[16]{0:T(128)S(1)} fusion(s32[4,8]{1,0:T(4,128)S(1)} %copy-done.2, s32[16]{0:T(128)S(1)} %fusion.47), kind=kCustom, calls=%fused_computation.1 | custom fusion | bytes 256 | tf_op jit(solution)/shard_map/gather | solution.py:104
  42.6 8.5 %all-to-all-done.1 = bf16[16,64,128]{2,1,0:T(8,128)(2,1)S(1)} async-done(((bf16[16,64,128]{2,1,0:T(8,128)(2,1)}), bf16[16,64,128]{2,1,0:T(8,128)(2,1)S(1)}, u32[]{:S(2)}, u32[]{:S(2)}) %all-to-all-start.1) | async-done | bytes 262176 | tf_op jit(solution)/shard_map/all_to_all | solution.py:100
  51.0 0.3 fusion
  51.3 0.7 %convert_element_type.88 = bf16[1,256,128]{2,1,0:T(8,128)(2,1)} reshape(bf16[4,8192]{1,0:T(4,128)(2,1)S(1)} %fusion) | data formatting | bytes 131072 | tf_op jit(solution)/shard_map/convert_element_type | solution.py:116
  (40 shorter events, 1.1 us)
Async XLA Ops:
  0.0 31.5 %copy-start = (bf16[1,8,64,128]{3,2,1,0:T(8,128)(2,1)S(1)}, bf16[1,8,64,128]{3,2,1,0:T(8,128)(2,1)}, u32[]{:S(2)}) copy-start(bf16[1,8,64,128]{3,2,1,0:T(8,128)(2,1)} %param.13) | copy-start | bytes 393220
  0.0 13.8 %collective-permute-start.1 = (bf16[1,64,128]{2,1,0:T(8,128)(2,1)}, bf16[1,64,128]{2,1,0:T(8,128)(2,1)S(1)}, u32[]{:S(2)}, u32[]{:S(2)}) collective-permute-start(bf16[1,64,128]{2,1,0:T(8,128)(2,1)} %param.12), channel_id=1, source_target_pairs={{1,0},{2,1},{3,2},{4,3},{5,4},{6,5},{7,6},{8,7},{9,8},{10,9},{11,1... | collective-permute-start | bytes 49160 | tf_op jit(solution)/shard_map/ppermute | solution.py:19
  1.4 12.5 %collective-permute-start = (bf16[1,64,128]{2,1,0:T(8,128)(2,1)}, bf16[1,64,128]{2,1,0:T(8,128)(2,1)S(1)}, u32[]{:S(2)}, u32[]{:S(2)}) collective-permute-start(bf16[1,64,128]{2,1,0:T(8,128)(2,1)} %param.12), channel_id=1, source_target_pairs={{0,1},{1,2},{2,3},{3,4},{4,5},{5,6},{6,7},{7,8},{8,9},{9,10},{10,1... | collective-permute-start | bytes 49160 | tf_op jit(solution)/shard_map/ppermute | solution.py:17
  5.1 0.9 %copy-start.7 = (f32[3,3,128]{2,1,0:T(4,128)S(1)}, f32[3,3,128]{2,1,0:T(4,128)}, u32[]{:S(2)}) copy-start(f32[3,3,128]{2,1,0:T(4,128)} %param.21) | copy-start | bytes 13828
  6.1 0.7 %copy-start.11 = (s32[16]{0:T(128)S(1)}, s32[16]{0:T(128)}, u32[]{:S(2)}) copy-start(s32[16]{0:T(128)} %param.16) | copy-start | bytes 196
  9.9 0.7 %copy-start.1 = (s32[4]{0:T(128)S(1)}, s32[4]{0:T(128)}, u32[]{:S(2)}) copy-start(s32[4]{0:T(128)} %param.14) | copy-start | bytes 52
  12.5 1.4 %copy-start.3 = (bf16[3,128,128]{2,1,0:T(8,128)(2,1)S(1)}, bf16[3,128,128]{2,1,0:T(8,128)(2,1)}, u32[]{:S(2)}) copy-start(bf16[3,128,128]{2,1,0:T(8,128)(2,1)} %param.17) | copy-start | bytes 294916
  13.8 0.7 %copy-start.6 = (bf16[1,64,128]{2,1,0:T(8,128)(2,1)S(1)}, bf16[1,64,128]{2,1,0:T(8,128)(2,1)}, u32[]{:S(2)}) copy-start(bf16[1,64,128]{2,1,0:T(8,128)(2,1)} %param.12) | copy-start | bytes 49156
  15.6 8.1 %copy-start.8 = (f32[3,128]{1,0:T(4,128)S(1)}, f32[3,128]{1,0:T(4,128)}, u32[]{:S(2)}) copy-start(f32[3,128]{1,0:T(4,128)} %param.20) | copy-start | bytes 4612
  15.6 15.0 %all-to-all-start = ((bf16[16,16,128]{2,1,0:T(8,128)(2,1)}), bf16[16,16,128]{2,1,0:T(8,128)(2,1)S(1)}, u32[]{:S(2)}, u32[]{:S(2)}) async-start(bf16[16,16,128]{2,1,0:T(8,128)(2,1)} %bitcast.45), calls=%async_computation | async-start | bytes 131072 | tf_op jit(solution)/shard_map/all_to_all | solution.py:92
  30.6 0.8 %copy-start.4 = (bf16[128,128]{1,0:T(8,128)(2,1)S(1)}, bf16[128,128]{1,0:T(8,128)(2,1)}, u32[]{:S(2)}) copy-start(bf16[128,128]{1,0:T(8,128)(2,1)} %param.18) | copy-start | bytes 98308
  31.3 0.8 %copy-start.5 = (bf16[128,128]{1,0:T(8,128)(2,1)S(1)}, bf16[128,128]{1,0:T(8,128)(2,1)}, u32[]{:S(2)}) copy-start(bf16[128,128]{1,0:T(8,128)(2,1)} %param.19) | copy-start | bytes 98308
  32.6 1.0 %copy-start.9 = (bf16[3,512,128]{2,1,0:T(8,128)(2,1)S(1)}, bf16[3,512,128]{2,1,0:T(8,128)(2,1)}, u32[]{:S(2)}) copy-start(bf16[3,512,128]{2,1,0:T(8,128)(2,1)} %param.23) | copy-start | bytes 1179652
  32.6 1.1 %copy-start.10 = (bf16[3,128,512]{2,1,0:T(8,128)(2,1)S(1)}, bf16[3,128,512]{2,1,0:T(8,128)(2,1)}, u32[]{:S(2)}) copy-start(bf16[3,128,512]{2,1,0:T(8,128)(2,1)} %param.22) | copy-start | bytes 1179652
  37.5 13.5 %all-to-all-start.1 = ((bf16[16,64,128]{2,1,0:T(8,128)(2,1)}), bf16[16,64,128]{2,1,0:T(8,128)(2,1)S(1)}, u32[]{:S(2)}, u32[]{:S(2)}) async-start(bf16[16,64,128]{2,1,0:T(8,128)(2,1)} %constant_dynamic-update-slice_fusion), calls=%async_computation.1 | async-start | bytes 524288 | tf_op jit(solution)/shard_map/all_to_all | solution.py:100
  41.1 0.7 %copy-start.2 = (s32[4,8]{1,0:T(4,128)S(1)}, s32[4,8]{1,0:T(4,128)}, u32[]{:S(2)}) copy-start(s32[4,8]{1,0:T(4,128)} %param.15) | copy-start | bytes 388
where the time goes:
time: 52.8 us; the launch traced here: 52 us
  starting transfers between devices  16.1 us (30%)
  waiting for transfers between devices  15.4 us (29%)
  local copies, waits for them, and re-layouts  10.3 us (20%)
  between operations  4.86 us (9%)
  matrix products  3.93 us (7%)
  other arithmetic  1.47 us (3%)
    all_to_all x1, waiting for transfers between devices, on_device(): lax.all_to_all(placed, 'frame', split_axis=0, concat_axis=0, tiled=True)  8.48 us
    all_to_all x1, starting transfers between devices, on_device(): lax.all_to_all(outgoing, 'frame', split_axis=0, concat_axis=0, tiled=True)  8.11 us
    all_to_all x1, waiting for transfers between devices, on_device(): lax.all_to_all(outgoing, 'frame', split_axis=0, concat_axis=0, tiled=True)  6.87 us
    unnamed x25, local copies, waits for them, and re-layouts  5.51 us
    all_to_all x1, starting transfers between devices, on_device(): lax.all_to_all(placed, 'frame', split_axis=0, concat_axis=0, tiled=True)  3.53 us
    ppermute x1, starting transfers between devices, padded_2(): lax.ppermute(tail, axis, [(i, (i + 1) % count) for i in range(ends)])  3.04 us
    dot_general x3, matrix products, refine_block(): jnp.dot(hidden, mlp_out[layer_id], preferred_element_type=jnp.float32)  1.83 us
    ppermute x1, starting transfers between devices, padded_2(): lax.ppermute(head, axis, [((i + 1) % count, i) for i in range(ends)])  1.41 us
  transfers between devices with their start and end apart: 4, of which 2 were waited for; matrix products, arithmetic and copies ran while one was open for 8% of the time, Pallas kernels for 0%

commit v1 on v0

--- a/solution.py
+++ b/solution.py
@@ -4,6 +4,17 @@
 from jax.sharding import PartitionSpec as P
 
 TILES = 4
+
+
+def in_blocks(x, dim, size):
+    before, after = (x.shape[:dim], x.shape[dim + 1 :])
+    return jnp.moveaxis(x.reshape(*before, size, -1, *after), dim, 0)
+
+
+def laid_out(parts, dim):
+    shape = list(parts.shape[1:])
+    shape[dim] *= parts.shape[0]
+    return jnp.moveaxis(parts, 0, dim).reshape(shape)
 
 
 def padded_2(cells, sides, width):
@@ -89,7 +100,14 @@
     )
     outgoing = jnp.dot(picker, tile_rows, preferred_element_type=jnp.float32).astype(jnp.bfloat16)
     outgoing = outgoing.reshape(frame_total, low_pos, channels)
-    gathered = lax.all_to_all(outgoing, "frame", split_axis=0, concat_axis=0, tiled=True)
+    size, here = (lax.axis_size("frame"), lax.axis_index("frame"))
+    blocks = in_blocks(outgoing, 0, size)
+    outs = [blocks[here]]
+    for step in range(1, size):
+        sent = blocks[here ^ step]
+        outs.append(lax.ppermute(sent, "frame", [(i_2, i_2 ^ step) for i_2 in range(size)]))
+    blocks = jnp.stack(outs)[here ^ jnp.arange(size)]
+    gathered = laid_out(blocks, 0)
     window_tiles = lax.dynamic_slice_in_dim(gathered, own_start, window_len, 0)
     cond = jnp.repeat(window_tiles, 4, axis=1)
     refined = refine(cond, noisy[0], cond_w, noise_w, gains, tconv, mlp_in, mlp_out)

time: 52.8 us -> 65.7 us (1.24)
  starting transfers between devices: 16.1 us -> 31.9 us
  waiting for transfers between devices: 15.4 us -> 12.9 us
    ppermute x0 -> x15, starting transfers between devices: none -> 23.9 us  [on_device(): lax.ppermute(sent, 'frame', [(i_2, i_2 ^ step) for i_2 in range(size)])]
    all_to_all x1 -> x0, starting transfers between devices: 8.11 us -> none  [on_device(): lax.all_to_all(outgoing, 'frame', split_axis=0, concat_axis=0, tiled=True)]
    all_to_all x1 -> x0, waiting for transfers between devices: 6.87 us -> none  [on_device(): lax.all_to_all(outgoing, 'frame', split_axis=0, concat_axis=0, tiled=True)]
    ppermute x0 -> x15, waiting for transfers between devices: none -> 4.44 us  [on_device(): lax.ppermute(sent, 'frame', [(i_2, i_2 ^ step) for i_2 in range(size)])]
    select_n x1, other arithmetic: 0.67 us -> 0.01 us  [on_device(): offset = own_index - starts[source_window]]
    unnamed x25 -> x40, local copies, waits for them, and re-layouts: 5.51 us -> 4.98 us
  transfers between devices with their start and end apart: 4 -> 18, of which waited for: 2 -> 4; matrix products, arithmetic and copies ran while one was open for 8% -> 6% of each run, Pallas kernels for 0% -> 0%
where the time goes in v1:
time: 65.7 us; the launch traced here: 65.1 us
  starting transfers between devices  31.9 us (49%)
  waiting for transfers between devices  12.9 us (20%)
  local copies, waits for them, and re-layouts  10.4 us (16%)
  between operations  5.05 us (8%)
  matrix products  3.97 us (6%)
  other arithmetic  0.83 us (1%)
    ppermute x15, starting transfers between devices, on_device(): lax.ppermute(sent, 'frame', [(i_2, i_2 ^ step) for i_2 in range(size)])  23.9 us
    all_to_all x1, waiting for transfers between devices, on_device(): lax.all_to_all(placed, 'frame', split_axis=0, concat_axis=0, tiled=True)  8.48 us
    unnamed x40, local copies, waits for them, and re-layouts  4.98 us
    ppermute x15, waiting for transfers between devices, on_device(): lax.ppermute(sent, 'frame', [(i_2, i_2 ^ step) for i_2 in range(size)])  4.44 us
    all_to_all x1, starting transfers between devices, on_device(): lax.all_to_all(placed, 'frame', split_axis=0, concat_axis=0, tiled=True)  3.53 us
    ppermute x1, starting transfers between devices, padded_2(): lax.ppermute(tail, axis, [(i, (i + 1) % count) for i in range(ends)])  3.04 us
    dot_general x3, matrix products, refine_block(): jnp.dot(hidden, mlp_out[layer_id], preferred_element_type=jnp.float32)  1.83 us
    ppermute x1, starting transfers between devices, padded_2(): lax.ppermute(head, axis, [((i + 1) % count, i) for i in range(ends)])  1.41 us
  transfers between devices with their start and end apart: 18, of which 4 were waited for; matrix products, arithmetic and copies ran while one was open for 6% of the time, Pallas kernels for 0%

profile of v1, /device:TPU:0, one launch (start us, length us, event | category | flops | bytes accessed | tf_op | source)
XLA Modules:
  0.0 65.1 jit_solution(11077521934064456043)
XLA Ops:
  0.0 1.4 %collective-permute-start.1 = (bf16[1,64,128]{2,1,0:T(8,128)(2,1)}, bf16[1,64,128]{2,1,0:T(8,128)(2,1)S(1)}, u32[]{:S(2)}, u32[]{:S(2)}) collective-permute-start(bf16[1,64,128]{2,1,0:T(8,128)(2,1)} %param.12), channel_id=1, source_target_pairs={{1,0},{2,1},{3,2},{4,3},{5,4},{6,5},{7,6},{8,7},{9,8},{10,9},{11,1... | collective-permute-start | bytes 49160 | tf_op jit(solution)/shard_map/ppermute | solution.py:30
  1.4 3.0 %collective-permute-start = (bf16[1,64,128]{2,1,0:T(8,128)(2,1)}, bf16[1,64,128]{2,1,0:T(8,128)(2,1)S(1)}, u32[]{:S(2)}, u32[]{:S(2)}) collective-permute-start(bf16[1,64,128]{2,1,0:T(8,128)(2,1)} %param.12), channel_id=1, source_target_pairs={{0,1},{1,2},{2,3},{3,4},{4,5},{5,6},{6,7},{7,8},{8,9},{9,10},{10,1... | collective-permute-start | bytes 49160 | tf_op jit(solution)/shard_map/ppermute | solution.py:28
  4.5 0.6 copy-done.11
  5.2 0.9 %fusion.29 = f32[64,128]{1,0:T(8,128)S(1)} fusion(bf16[3,128,128]{2,1,0:T(8,128)(2,1)} %param.17, bf16[1,64,128]{2,1,0:T(8,128)(2,1)} %param.12), kind=kOutput, calls=%fused_computation.61 | convolution fusion | flops 2097152 | bytes 81920 | tf_op jit(solution)/shard_map/dot_general | solution.py:91
  7.5 2.7 %collective-permute-start.2 = (bf16[1,16,128]{2,1,0:T(8,128)(2,1)S(1)}, bf16[1,16,128]{2,1,0:T(8,128)(2,1)S(1)}, u32[]{:S(2)}, u32[]{:S(2)}) collective-permute-start(bf16[1,16,128]{2,1,0:T(8,128)(2,1)S(1)} %get-tuple-element.55), channel_id=1, source_target_pairs={{0,1},{1,0},{2,3},{3,2},{4,5},{5,4},{6,7},{7,6},{8,9},{9,8},{10,11... | collective-permute-start | bytes 12296 | tf_op jit(solution)/shard_map/ppermute | solution.py:108
  10.2 0.6 dynamic_slice.80
  13.4 0.6 copy-done.1
  14.0 0.6 dynamic_slice.81
  15.9 0.7 %gather_fusion = s32[16]{0:T(128)S(1)} fusion(s32[4]{0:T(128)S(1)} %copy-done.1, s32[1024]{0:T(1024)S(1)} %pad_clamp_fusion.1), kind=kCustom, calls=%fused_computation | custom fusion | bytes 192 | tf_op jit(solution)/shard_map/gather | solution.py:119
  17.2 2.4 %collective-permute-start.3 = (bf16[1,16,128]{2,1,0:T(8,128)(2,1)S(1)}, bf16[1,16,128]{2,1,0:T(8,128)(2,1)S(1)}, u32[]{:S(2)}, u32[]{:S(2)}) collective-permute-start(bf16[1,16,128]{2,1,0:T(8,128)(2,1)S(1)} %get-tuple-element.54), channel_id=1, source_target_pairs={{0,2},{1,3},{2,0},{3,1},{4,6},{5,7},{6,4},{7,5},{8,10},{9,11},{10,... | collective-permute-start | bytes 12296 | tf_op jit(solution)/shard_map/ppermute | solution.py:108
  19.6 2.0 %collective-permute-start.5 = (bf16[1,16,128]{2,1,0:T(8,128)(2,1)S(1)}, bf16[1,16,128]{2,1,0:T(8,128)(2,1)S(1)}, u32[]{:S(2)}, u32[]{:S(2)}) collective-permute-start(bf16[1,16,128]{2,1,0:T(8,128)(2,1)S(1)} %get-tuple-element.52), channel_id=1, source_target_pairs={{0,4},{1,5},{2,6},{3,7},{4,0},{5,1},{6,2},{7,3},{8,12},{9,13},{10,... | collective-permute-start | bytes 12296 | tf_op jit(solution)/shard_map/ppermute | solution.py:108
  21.7 2.5 %collective-permute-start.7 = (bf16[1,16,128]{2,1,0:T(8,128)(2,1)S(1)}, bf16[1,16,128]{2,1,0:T(8,128)(2,1)S(1)}, u32[]{:S(2)}, u32[]{:S(2)}) collective-permute-start(bf16[1,16,128]{2,1,0:T(8,128)(2,1)S(1)} %get-tuple-element.50), channel_id=1, source_target_pairs={{0,6},{1,7},{2,4},{3,5},{4,2},{5,3},{6,0},{7,1},{8,14},{9,15},{10,... | collective-permute-start | bytes 12296 | tf_op jit(solution)/shard_map/ppermute | solution.py:108
  24.2 2.9 %collective-permute-start.9 = (bf16[1,16,128]{2,1,0:T(8,128)(2,1)S(1)}, bf16[1,16,128]{2,1,0:T(8,128)(2,1)S(1)}, u32[]{:S(2)}, u32[]{:S(2)}) collective-permute-start(bf16[1,16,128]{2,1,0:T(8,128)(2,1)S(1)} %get-tuple-element.48), channel_id=1, source_target_pairs={{0,8},{1,9},{2,10},{3,11},{4,12},{5,13},{6,14},{7,15},{8,0},{9,1},... | collective-permute-start | bytes 12296 | tf_op jit(solution)/shard_map/ppermute | solution.py:108
  27.1 3.4 %collective-permute-start.11 = (bf16[1,16,128]{2,1,0:T(8,128)(2,1)S(1)}, bf16[1,16,128]{2,1,0:T(8,128)(2,1)S(1)}, u32[]{:S(2)}, u32[]{:S(2)}) collective-permute-start(bf16[1,16,128]{2,1,0:T(8,128)(2,1)S(1)} %get-tuple-element.46), channel_id=1, source_target_pairs={{0,10},{1,11},{2,8},{3,9},{4,14},{5,15},{6,12},{7,13},{8,2},{9,3},... | collective-permute-start | bytes 12296 | tf_op jit(solution)/shard_map/ppermute | solution.py:108
  30.5 3.8 %collective-permute-start.13 = (bf16[1,16,128]{2,1,0:T(8,128)(2,1)S(1)}, bf16[1,16,128]{2,1,0:T(8,128)(2,1)S(1)}, u32[]{:S(2)}, u32[]{:S(2)}) collective-permute-start(bf16[1,16,128]{2,1,0:T(8,128)(2,1)S(1)} %get-tuple-element.44), channel_id=1, source_target_pairs={{0,12},{1,13},{2,14},{3,15},{4,8},{5,9},{6,10},{7,11},{8,4},{9,5},... | collective-permute-start | bytes 12296 | tf_op jit(solution)/shard_map/ppermute | solution.py:108
  34.4 3.0 %collective-permute-start.15 = (bf16[1,16,128]{2,1,0:T(8,128)(2,1)S(1)}, bf16[1,16,128]{2,1,0:T(8,128)(2,1)S(1)}, u32[]{:S(2)}, u32[]{:S(2)}) collective-permute-start(bf16[1,16,128]{2,1,0:T(8,128)(2,1)S(1)} %get-tuple-element.40), channel_id=1, source_target_pairs={{0,14},{1,15},{2,12},{3,13},{4,10},{5,11},{6,8},{7,9},{8,6},{9,7},... | collective-permute-start | bytes 12296 | tf_op jit(solution)/shard_map/ppermute | solution.py:108
  37.4 1.3 %collective-permute-start.16 = (bf16[1,16,128]{2,1,0:T(8,128)(2,1)S(1)}, bf16[1,16,128]{2,1,0:T(8,128)(2,1)S(1)}, u32[]{:S(2)}, u32[]{:S(2)}) collective-permute-start(bf16[1,16,128]{2,1,0:T(8,128)(2,1)S(1)} %get-tuple-element.29), channel_id=1, source_target_pairs={{0,15},{1,14},{2,13},{3,12},{4,11},{5,10},{6,9},{7,8},{8,7},{9,6},... | collective-permute-start | bytes 12296 | tf_op jit(solution)/shard_map/ppermute | solution.py:108
  39.2 1.6 %collective-permute-done.15 = bf16[1,16,128]{2,1,0:T(8,128)(2,1)S(1)} collective-permute-done((bf16[1,16,128]{2,1,0:T(8,128)(2,1)S(1)}, bf16[1,16,128]{2,1,0:T(8,128)(2,1)S(1)}, u32[]{:S(2)}, u32[]{:S(2)}) %collective-permute-start.15) | collective-permute-done | bytes 4128 | tf_op jit(solution)/shard_map/ppermute | solution.py:108
  40.7 2.3 %collective-permute-done.16 = bf16[1,16,128]{2,1,0:T(8,128)(2,1)S(1)} collective-permute-done((bf16[1,16,128]{2,1,0:T(8,128)(2,1)S(1)}, bf16[1,16,128]{2,1,0:T(8,128)(2,1)S(1)}, u32[]{:S(2)}, u32[]{:S(2)}) %collective-permute-start.16) | collective-permute-done | bytes 4128 | tf_op jit(solution)/shard_map/ppermute | solution.py:108
  43.1 0.6 gather_fusion.2
  43.7 0.7 %copy-done.4 = bf16[128,128]{1,0:T(8,128)(2,1)S(1)} copy-done((bf16[128,128]{1,0:T(8,128)(2,1)S(1)}, bf16[128,128]{1,0:T(8,128)(2,1)}, u32[]{:S(2)}) %copy-start.4) | copy-done | bytes 32792
  44.6 0.6 copy-done.5
  45.8 0.9 %copy-done.9 = bf16[3,512,128]{2,1,0:T(8,128)(2,1)S(1)} copy-done((bf16[3,512,128]{2,1,0:T(8,128)(2,1)S(1)}, bf16[3,512,128]{2,1,0:T(8,128)(2,1)}, u32[]{:S(2)}) %copy-start.9) | copy-done | bytes 393240
  46.8 0.6 multiply_reduce_fusion.1
  47.7 0.6 multiply_reduce_fusion
  49.2 0.8 %broadcast_in_dim.17 = bf16[16,64,128]{2,1,0:T(8,128)(2,1)} broadcast(bf16[]{:T(256)} %constant.101.clone.1), dimensions={} | broadcast | bytes 262146 | tf_op jit(solution)/shard_map/broadcast_in_dim | solution.py:116
  50.0 0.6 constant_dynamic-update-slice_fusion.16
  50.6 3.5 %all-to-all-start = ((bf16[16,64,128]{2,1,0:T(8,128)(2,1)}), bf16[16,64,128]{2,1,0:T(8,128)(2,1)S(1)}, u32[]{:S(2)}, u32[]{:S(2)}) async-start(bf16[16,64,128]{2,1,0:T(8,128)(2,1)} %constant_dynamic-update-slice_fusion.16), calls=%async_computation | async-start | bytes 524288 | tf_op jit(solution)/shard_map/all_to_all | solution.py:118
  54.2 0.7 %copy-done.2 = s32[4,8]{1,0:T(4,128)S(1)} copy-done((s32[4,8]{1,0:T(4,128)S(1)}, s32[4,8]{1,0:T(4,128)}, u32[]{:S(2)}) %copy-start.2) | copy-done | bytes 152
  54.9 0.7 %gather_fusion.1 = s32[16]{0:T(128)S(1)} fusion(s32[4,8]{1,0:T(4,128)S(1)} %copy-done.2, s32[16]{0:T(128)S(1)} %fusion.63), kind=kCustom, calls=%fused_computation.1 | custom fusion | bytes 256 | tf_op jit(solution)/shard_map/gather | solution.py:122
  55.7 8.5 %all-to-all-done = bf16[16,64,128]{2,1,0:T(8,128)(2,1)S(1)} async-done(((bf16[16,64,128]{2,1,0:T(8,128)(2,1)}), bf16[16,64,128]{2,1,0:T(8,128)(2,1)S(1)}, u32[]{:S(2)}, u32[]{:S(2)}) %all-to-all-start) | async-done | bytes 262176 | tf_op jit(solution)/shard_map/all_to_all | solution.py:118
  64.4 0.7 %convert_element_type.88 = bf16[1,256,128]{2,1,0:T(8,128)(2,1)} reshape(bf16[4,8192]{1,0:T(4,128)(2,1)S(1)} %fusion) | data formatting | bytes 131072 | tf_op jit(solution)/shard_map/convert_element_type | solution.py:134
  (87 shorter events, 4.3 us)
Async XLA Ops:
  0.0 44.6 %copy-start = (bf16[1,8,64,128]{3,2,1,0:T(8,128)(2,1)S(1)}, bf16[1,8,64,128]{3,2,1,0:T(8,128)(2,1)}, u32[]{:S(2)}) copy-start(bf16[1,8,64,128]{3,2,1,0:T(8,128)(2,1)} %param.13) | copy-start | bytes 393220
  0.0 6.3 %collective-permute-start.1 = (bf16[1,64,128]{2,1,0:T(8,128)(2,1)}, bf16[1,64,128]{2,1,0:T(8,128)(2,1)S(1)}, u32[]{:S(2)}, u32[]{:S(2)}) collective-permute-start(bf16[1,64,128]{2,1,0:T(8,128)(2,1)} %param.12), channel_id=1, source_target_pairs={{1,0},{2,1},{3,2},{4,3},{5,4},{6,5},{7,6},{8,7},{9,8},{10,9},{11,1... | collective-permute-start | bytes 49160 | tf_op jit(solution)/shard_map/ppermute | solution.py:30
  1.4 5.0 %collective-permute-start = (bf16[1,64,128]{2,1,0:T(8,128)(2,1)}, bf16[1,64,128]{2,1,0:T(8,128)(2,1)S(1)}, u32[]{:S(2)}, u32[]{:S(2)}) collective-permute-start(bf16[1,64,128]{2,1,0:T(8,128)(2,1)} %param.12), channel_id=1, source_target_pairs={{0,1},{1,2},{2,3},{3,4},{4,5},{5,6},{6,7},{7,8},{8,9},{9,10},{10,1... | collective-permute-start | bytes 49160 | tf_op jit(solution)/shard_map/ppermute | solution.py:28
  4.5 0.7 %copy-start.11 = (s32[16]{0:T(128)S(1)}, s32[16]{0:T(128)}, u32[]{:S(2)}) copy-start(s32[16]{0:T(128)} %param.16) | copy-start | bytes 196
  5.1 1.0 %copy-start.8 = (f32[3,128]{1,0:T(4,128)S(1)}, f32[3,128]{1,0:T(4,128)}, u32[]{:S(2)}) copy-start(f32[3,128]{1,0:T(4,128)} %param.20) | copy-start | bytes 4612
  5.1 1.0 %copy-start.7 = (f32[3,3,128]{2,1,0:T(4,128)S(1)}, f32[3,3,128]{2,1,0:T(4,128)}, u32[]{:S(2)}) copy-start(f32[3,3,128]{2,1,0:T(4,128)} %param.21) | copy-start | bytes 13828
  5.1 1.1 %copy-start.3 = (bf16[3,128,128]{2,1,0:T(8,128)(2,1)S(1)}, bf16[3,128,128]{2,1,0:T(8,128)(2,1)}, u32[]{:S(2)}) copy-start(bf16[3,128,128]{2,1,0:T(8,128)(2,1)} %param.17) | copy-start | bytes 294916
  6.3 0.7 %copy-start.6 = (bf16[1,64,128]{2,1,0:T(8,128)(2,1)S(1)}, bf16[1,64,128]{2,1,0:T(8,128)(2,1)}, u32[]{:S(2)}) copy-start(bf16[1,64,128]{2,1,0:T(8,128)(2,1)} %param.12) | copy-start | bytes 49156
  7.5 14.2 %collective-permute-start.2 = (bf16[1,16,128]{2,1,0:T(8,128)(2,1)S(1)}, bf16[1,16,128]{2,1,0:T(8,128)(2,1)S(1)}, u32[]{:S(2)}, u32[]{:S(2)}) collective-permute-start(bf16[1,16,128]{2,1,0:T(8,128)(2,1)S(1)} %get-tuple-element.55), channel_id=1, source_target_pairs={{0,1},{1,0},{2,3},{3,2},{4,5},{5,4},{6,7},{7,6},{8,9},{9,8},{10,11... | collective-permute-start | bytes 12296 | tf_op jit(solution)/shard_map/ppermute | solution.py:108
  13.3 0.7 %copy-start.1 = (s32[4]{0:T(128)S(1)}, s32[4]{0:T(128)}, u32[]{:S(2)}) copy-start(s32[4]{0:T(128)} %param.14) | copy-start | bytes 52
  17.2 6.9 %collective-permute-start.3 = (bf16[1,16,128]{2,1,0:T(8,128)(2,1)S(1)}, bf16[1,16,128]{2,1,0:T(8,128)(2,1)S(1)}, u32[]{:S(2)}, u32[]{:S(2)}) collective-permute-start(bf16[1,16,128]{2,1,0:T(8,128)(2,1)S(1)} %get-tuple-element.54), channel_id=1, source_target_pairs={{0,2},{1,3},{2,0},{3,1},{4,6},{5,7},{6,4},{7,5},{8,10},{9,11},{10,... | collective-permute-start | bytes 12296 | tf_op jit(solution)/shard_map/ppermute | solution.py:108
  19.6 4.5 %collective-permute-start.4 = (bf16[1,16,128]{2,1,0:T(8,128)(2,1)S(1)}, bf16[1,16,128]{2,1,0:T(8,128)(2,1)S(1)}, u32[]{:S(2)}, u32[]{:S(2)}) collective-permute-start(bf16[1,16,128]{2,1,0:T(8,128)(2,1)S(1)} %get-tuple-element.53), channel_id=1, source_target_pairs={{0,3},{1,2},{2,1},{3,0},{4,7},{5,6},{6,5},{7,4},{8,11},{9,10},{10,... | collective-permute-start | bytes 12296 | tf_op jit(solution)/shard_map/ppermute | solution.py:108
  19.6 7.5 %collective-permute-start.5 = (bf16[1,16,128]{2,1,0:T(8,128)(2,1)S(1)}, bf16[1,16,128]{2,1,0:T(8,128)(2,1)S(1)}, u32[]{:S(2)}, u32[]{:S(2)}) collective-permute-start(bf16[1,16,128]{2,1,0:T(8,128)(2,1)S(1)} %get-tuple-element.52), channel_id=1, source_target_pairs={{0,4},{1,5},{2,6},{3,7},{4,0},{5,1},{6,2},{7,3},{8,12},{9,13},{10,... | collective-permute-start | bytes 12296 | tf_op jit(solution)/shard_map/ppermute | solution.py:108
  21.7 5.5 %collective-permute-start.6 = (bf16[1,16,128]{2,1,0:T(8,128)(2,1)S(1)}, bf16[1,16,128]{2,1,0:T(8,128)(2,1)S(1)}, u32[]{:S(2)}, u32[]{:S(2)}) collective-permute-start(bf16[1,16,128]{2,1,0:T(8,128)(2,1)S(1)} %get-tuple-element.51), channel_id=1, source_target_pairs={{0,5},{1,4},{2,7},{3,6},{4,1},{5,0},{6,3},{7,2},{8,13},{9,12},{10,... | collective-permute-start | bytes 12296 | tf_op jit(solution)/shard_map/ppermute | solution.py:108
  21.7 8.8 %collective-permute-start.7 = (bf16[1,16,128]{2,1,0:T(8,128)(2,1)S(1)}, bf16[1,16,128]{2,1,0:T(8,128)(2,1)S(1)}, u32[]{:S(2)}, u32[]{:S(2)}) collective-permute-start(bf16[1,16,128]{2,1,0:T(8,128)(2,1)S(1)} %get-tuple-element.50), channel_id=1, source_target_pairs={{0,6},{1,7},{2,4},{3,5},{4,2},{5,3},{6,0},{7,1},{8,14},{9,15},{10,... | collective-permute-start | bytes 12296 | tf_op jit(solution)/shard_map/ppermute | solution.py:108
  24.1 6.4 %collective-permute-start.8 = (bf16[1,16,128]{2,1,0:T(8,128)(2,1)S(1)}, bf16[1,16,128]{2,1,0:T(8,128)(2,1)S(1)}, u32[]{:S(2)}, u32[]{:S(2)}) collective-permute-start(bf16[1,16,128]{2,1,0:T(8,128)(2,1)S(1)} %get-tuple-element.49), channel_id=1, source_target_pairs={{0,7},{1,6},{2,5},{3,4},{4,3},{5,2},{6,1},{7,0},{8,15},{9,14},{10,... | collective-permute-start | bytes 12296 | tf_op jit(solution)/shard_map/ppermute | solution.py:108
  24.2 10.2 %collective-permute-start.9 = (bf16[1,16,128]{2,1,0:T(8,128)(2,1)S(1)}, bf16[1,16,128]{2,1,0:T(8,128)(2,1)S(1)}, u32[]{:S(2)}, u32[]{:S(2)}) collective-permute-start(bf16[1,16,128]{2,1,0:T(8,128)(2,1)S(1)} %get-tuple-element.48), channel_id=1, source_target_pairs={{0,8},{1,9},{2,10},{3,11},{4,12},{5,13},{6,14},{7,15},{8,0},{9,1},... | collective-permute-start | bytes 12296 | tf_op jit(solution)/shard_map/ppermute | solution.py:108
  27.1 7.3 %collective-permute-start.10 = (bf16[1,16,128]{2,1,0:T(8,128)(2,1)S(1)}, bf16[1,16,128]{2,1,0:T(8,128)(2,1)S(1)}, u32[]{:S(2)}, u32[]{:S(2)}) collective-permute-start(bf16[1,16,128]{2,1,0:T(8,128)(2,1)S(1)} %get-tuple-element.47), channel_id=1, source_target_pairs={{0,9},{1,8},{2,11},{3,10},{4,13},{5,12},{6,15},{7,14},{8,1},{9,0},... | collective-permute-start | bytes 12296 | tf_op jit(solution)/shard_map/ppermute | solution.py:108
  27.1 10.2 %collective-permute-start.11 = (bf16[1,16,128]{2,1,0:T(8,128)(2,1)S(1)}, bf16[1,16,128]{2,1,0:T(8,128)(2,1)S(1)}, u32[]{:S(2)}, u32[]{:S(2)}) collective-permute-start(bf16[1,16,128]{2,1,0:T(8,128)(2,1)S(1)} %get-tuple-element.46), channel_id=1, source_target_pairs={{0,10},{1,11},{2,8},{3,9},{4,14},{5,15},{6,12},{7,13},{8,2},{9,3},... | collective-permute-start | bytes 12296 | tf_op jit(solution)/shard_map/ppermute | solution.py:108
  30.5 8.1 %collective-permute-start.12 = (bf16[1,16,128]{2,1,0:T(8,128)(2,1)S(1)}, bf16[1,16,128]{2,1,0:T(8,128)(2,1)S(1)}, u32[]{:S(2)}, u32[]{:S(2)}) collective-permute-start(bf16[1,16,128]{2,1,0:T(8,128)(2,1)S(1)} %get-tuple-element.45), channel_id=1, source_target_pairs={{0,11},{1,10},{2,9},{3,8},{4,15},{5,14},{6,13},{7,12},{8,3},{9,2},... | collective-permute-start | bytes 12296 | tf_op jit(solution)/shard_map/ppermute | solution.py:108
  30.5 8.1 %collective-permute-start.13 = (bf16[1,16,128]{2,1,0:T(8,128)(2,1)S(1)}, bf16[1,16,128]{2,1,0:T(8,128)(2,1)S(1)}, u32[]{:S(2)}, u32[]{:S(2)}) collective-permute-start(bf16[1,16,128]{2,1,0:T(8,128)(2,1)S(1)} %get-tuple-element.44), channel_id=1, source_target_pairs={{0,12},{1,13},{2,14},{3,15},{4,8},{5,9},{6,10},{7,11},{8,4},{9,5},... | collective-permute-start | bytes 12296 | tf_op jit(solution)/shard_map/ppermute | solution.py:108
  34.3 4.8 %collective-permute-start.14 = (bf16[1,16,128]{2,1,0:T(8,128)(2,1)S(1)}, bf16[1,16,128]{2,1,0:T(8,128)(2,1)S(1)}, u32[]{:S(2)}, u32[]{:S(2)}) collective-permute-start(bf16[1,16,128]{2,1,0:T(8,128)(2,1)S(1)} %get-tuple-element.42), channel_id=1, source_target_pairs={{0,13},{1,12},{2,15},{3,14},{4,9},{5,8},{6,11},{7,10},{8,5},{9,4},... | collective-permute-start | bytes 12296 | tf_op jit(solution)/shard_map/ppermute | solution.py:108
  34.4 6.4 %collective-permute-start.15 = (bf16[1,16,128]{2,1,0:T(8,128)(2,1)S(1)}, bf16[1,16,128]{2,1,0:T(8,128)(2,1)S(1)}, u32[]{:S(2)}, u32[]{:S(2)}) collective-permute-start(bf16[1,16,128]{2,1,0:T(8,128)(2,1)S(1)} %get-tuple-element.40), channel_id=1, source_target_pairs={{0,14},{1,15},{2,12},{3,13},{4,10},{5,11},{6,8},{7,9},{8,6},{9,7},... | collective-permute-start | bytes 12296 | tf_op jit(solution)/shard_map/ppermute | solution.py:108
  37.4 5.7 %collective-permute-start.16 = (bf16[1,16,128]{2,1,0:T(8,128)(2,1)S(1)}, bf16[1,16,128]{2,1,0:T(8,128)(2,1)S(1)}, u32[]{:S(2)}, u32[]{:S(2)}) collective-permute-start(bf16[1,16,128]{2,1,0:T(8,128)(2,1)S(1)} %get-tuple-element.29), channel_id=1, source_target_pairs={{0,15},{1,14},{2,13},{3,12},{4,11},{5,10},{6,9},{7,8},{8,7},{9,6},... | collective-permute-start | bytes 12296 | tf_op jit(solution)/shard_map/ppermute | solution.py:108
  43.7 0.8 %copy-start.4 = (bf16[128,128]{1,0:T(8,128)(2,1)S(1)}, bf16[128,128]{1,0:T(8,128)(2,1)}, u32[]{:S(2)}) copy-start(bf16[128,128]{1,0:T(8,128)(2,1)} %param.18) | copy-start | bytes 98308
  44.4 0.8 %copy-start.5 = (bf16[128,128]{1,0:T(8,128)(2,1)S(1)}, bf16[128,128]{1,0:T(8,128)(2,1)}, u32[]{:S(2)}) copy-start(bf16[128,128]{1,0:T(8,128)(2,1)} %param.19) | copy-start | bytes 98308
  45.7 1.0 %copy-start.9 = (bf16[3,512,128]{2,1,0:T(8,128)(2,1)S(1)}, bf16[3,512,128]{2,1,0:T(8,128)(2,1)}, u32[]{:S(2)}) copy-start(bf16[3,512,128]{2,1,0:T(8,128)(2,1)} %param.23) | copy-start | bytes 1179652
  45.7 1.1 %copy-start.10 = (bf16[3,128,512]{2,1,0:T(8,128)(2,1)S(1)}, bf16[3,128,512]{2,1,0:T(8,128)(2,1)}, u32[]{:S(2)}) copy-start(bf16[3,128,512]{2,1,0:T(8,128)(2,1)} %param.22) | copy-start | bytes 1179652
  50.6 13.5 %all-to-all-start = ((bf16[16,64,128]{2,1,0:T(8,128)(2,1)}), bf16[16,64,128]{2,1,0:T(8,128)(2,1)S(1)}, u32[]{:S(2)}, u32[]{:S(2)}) async-start(bf16[16,64,128]{2,1,0:T(8,128)(2,1)} %constant_dynamic-update-slice_fusion.16), calls=%async_computation | async-start | bytes 524288 | tf_op jit(solution)/shard_map/all_to_all | solution.py:118
  54.2 0.7 %copy-start.2 = (s32[4,8]{1,0:T(4,128)S(1)}, s32[4,8]{1,0:T(4,128)}, u32[]{:S(2)}) copy-start(s32[4,8]{1,0:T(4,128)} %param.15) | copy-start | bytes 388
